TPU v7x, 32 devices: a whole 2x2x4 slice. The times are simulated.
32 devices in a mesh: grp: 4 (over z), inner: 8 (over y, x, core).
Axes of the slice: x: 2, y: 2, z: 4, core: 2. Of those that a mesh axis runs over, the one named last changes fastest.
Arguments:
- design: float32 [8, 4096, 1024], P('inner', 'grp'), may hold values from -6 to 6
- row_signs: int32 [8, 4096], P('inner', 'grp'), may hold values from 0 to 1
- kept_rows: int32 [8, 2048], P('inner'), may hold values from 0 to 4095, as said below
Outputs:
- factored: float32 [2048, 1024], P('grp')
Inputs may be any that keep to these rules, and one draw needn't show every extreme that they name: `kept_rows`: within each block the 2048 kept row numbers are distinct, and each block keeps its first and its last row.
All inputs are finite; a program needn't handle non-finite values.
Results may differ from a plain program's by a relative error of at most 0.0048.
Values may be sent and summed in bfloat16 or wider, within the bound.
No kernel may reach another device: no remote copies, remote signals or barrier semaphores. Data moves between devices by JAX's collectives and lax.ppermute only.
A program may use at most 64 MiB of HBM per device.

v0:
```python
import math
import jax
import jax.numpy as jnp
from jax import lax
from jax.sharding import PartitionSpec as P

COLS_DONE = 8
epsilon = 1e-06


def sign_table(row_ids, col_ids):
    common_bits = jnp.bitwise_and(row_ids[:, None], col_ids[None, :])
    ones_total = jnp.zeros(common_bits.shape, jnp.int32)
    for bit_pos in range(4):
        ones_total = ones_total + jnp.bitwise_and(jnp.right_shift(common_bits, bit_pos), 1)
    return 1.0 - 2.0 * jnp.bitwise_and(ones_total, 1).astype(jnp.float32)


def pick_rows(table_rows, chosen_rows):
    return jnp.take(table_rows, chosen_rows, axis=0)


def on_device(design, row_signs, kept_rows):
    block_count, local_rows, columns = design.shape
    keep_count = kept_rows.shape[1]
    groups = lax.axis_size("grp")
    owned_rows = keep_count // groups
    highest = lax.Precision.HIGHEST
    sixteen = jnp.arange(16, dtype=jnp.int32)
    hadamard = sign_table(sixteen, sixteen).astype(jnp.bfloat16)
    flipped = (design * (1 - 2 * row_signs).astype(jnp.float32)[:, :, None]).astype(jnp.bfloat16)
    lowest = flipped.reshape(block_count * local_rows // 16, 16, columns)
    first_pass = jnp.einsum(
        "hc,ncd->nhd", hadamard, lowest, preferred_element_type=jnp.float32
    ).astype(jnp.bfloat16)
    middle_view = first_pass.reshape(block_count * local_rows // 256, 16, 16, columns)
    second_pass = jnp.einsum(
        "hb,mbcd->mhcd", hadamard, middle_view, preferred_element_type=jnp.float32
    ).astype(jnp.bfloat16)
    second_pass = second_pass.reshape(block_count, local_rows, columns)
    gathered_rows = lax.all_to_all(second_pass, "grp", split_axis=2, concat_axis=1, tiled=True)
    col_count = gathered_rows.shape[2]
    by_piece = gathered_rows.reshape(block_count, 16, 256, col_count)
    mixed_rows = jnp.einsum("ha,nakd->nhkd", hadamard, by_piece, preferred_element_type=jnp.float32)
    mixed_rows = mixed_rows.reshape(block_count, 16 * 256, col_count)
    picked = jax.vmap(pick_rows)(mixed_rows, kept_rows)
    partial_value = jnp.sum(picked, axis=0)
    summed = lax.psum(partial_value, "inner")
    sketch = lax.all_to_all(summed, "grp", split_axis=0, concat_axis=1, tiled=True)
    sketch = sketch * (1.0 / (64.0 * math.sqrt(keep_count)))
    row_base = lax.axis_index("grp") * owned_rows
    global_rows = row_base + jnp.arange(owned_rows, dtype=jnp.int32)

    def reflect(col_index, current):
        column = jnp.where(global_rows >= col_index, current[:, col_index], 0.0)
        is_pivot = (global_rows == col_index).astype(jnp.float32)
        norm_sq, crossed, pivot_row = lax.psum(
            (
                jnp.sum(column * column),
                jnp.dot(column, current, precision=highest),
                jnp.dot(is_pivot, current, precision=highest),
            ),
            "grp",
        )
        pivot_value = pivot_row[col_index]
        head_value = -jnp.where(pivot_value >= 0, 1.0, -1.0) * jnp.sqrt(norm_sq)
        length = 2.0 * (norm_sq - head_value * pivot_value) + epsilon
        projected_row = crossed - head_value * pivot_row
        vector = column - head_value * is_pivot
        return current - vector[:, None] * (2.0 * projected_row / length)[None, :]

    result = lax.fori_loop(0, COLS_DONE, reflect, sketch)
    return result


def solution(mesh):
    return jax.shard_map(
        on_device,
        mesh=mesh,
        in_specs=(P("inner", "grp", None), P("inner", "grp"), P("inner", None)),
        out_specs=P("grp", None),
        check_vma=False,
    )
```

profile of v0, /device:TPU:0, one launch (start us, length us, event | category | flops | bytes accessed | tf_op | source)
XLA Modules:
  0.0 397.2 jit_solution(10092679646443896874)
XLA Ops:
  6.5 0.7 subtract_convert_fusion.4
  7.2 2.5 multiply_convert_fusion
  9.7 0.7 convolution_convert_fusion
  10.4 1.5 convert_bitcast_fusion
  11.9 1.2 copy.21
  13.1 7.7 %copy.22 = bf16[1,1024,1024]{1,0,2:T(2,128)(2,1)} copy(bf16[1,1024,1024]{2,1,0:T(8,128)(2,1)S(1)} %bitcast.77) | data formatting | bytes 4194304 | tf_op jit(solution)/shard_map/reshape | solution.py:40
  21.4 12.8 %reduce.2 = bf16[1024,1024]{1,0:T(8,128)(2,1)S(1)} reduce(bf16[1024,1,1024]{2,1,0:T(2,128)(2,1)} %bitcast.75, bf16[]{:T(256)} %broadcast.106), dimensions={1}, to_apply=%bitcast.43.reduce_sub_computation | reduce | bytes 4194306
  34.2 2.8 reshape.93
  36.9 6.5 %all-to-all-start = ((bf16[4,2,131072]{2,1,0:T(2,128)(2,1)}), bf16[4,2,131072]{2,1,0:T(2,128)(2,1)S(1)}, u32[]{:S(2)}, u32[]{:S(2)}) async-start(bf16[4,2,131072]{2,1,0:T(2,128)(2,1)} %reshape.93), calls=%async_computation | async-start | bytes 4194304 | tf_op jit(solution)/shard_map/all_to_all | solution.py:41
  43.5 48.1 %all-to-all-done = bf16[4,2,131072]{2,1,0:T(2,128)(2,1)S(1)} async-done(((bf16[4,2,131072]{2,1,0:T(2,128)(2,1)}), bf16[4,2,131072]{2,1,0:T(2,128)(2,1)S(1)}, u32[]{:S(2)}, u32[]{:S(2)}) %all-to-all-start) | async-done | bytes 2097184 | tf_op jit(solution)/shard_map/all_to_all | solution.py:41
  91.6 3.4 reshape.94
  94.9 3.0 copy.29
  97.9 2.6 copy.23
  100.5 2.9 convolution_bitcast_fusion
  103.4 4.4 %copy.25 = f32[1,16,256,256]{3,2,1,0:T(8,128)} copy(f32[1,16,256,256]{3,1,2,0:T(8,128)S(1)} %convolution_bitcast_fusion) | data formatting | bytes 8388608 | tf_op jit(solution)/shard_map/ha,nakd->nhkd/transpose | solution.py:44
  107.8 21.4 %gather_fusion = f32[2048,256]{1,0:T(8,128)S(1)} fusion(f32[1,4096,256]{2,1,0:T(8,128)} %bitcast.74, s32[2048]{0:T(1024)S(1)} %bitcast.73), kind=kCustom, calls=%fused_computation | custom fusion | bytes 4210688 | tf_op jit(solution)/shard_map/vmap(jit(_take))/gather | solution.py:20
  129.2 1.7 broadcast_select_fusion.2
  130.8 61.1 %all-reduce.5.cloned.1.call-done = f32[4,512,256]{2,1,0:T(8,128)} async-done(((f32[4,512,256]{2,1,0:T(8,128)}), f32[4,512,256]{2,1,0:T(8,128)}) %all-reduce.5.cloned.1.call-update) | async-done | bytes 2097168 | tf_op jit(solution)/shard_map/psum | solution.py:48
  191.9 4.5 %all-to-all-start.1 = ((f32[4,512,256]{2,1,0:T(8,128)}), f32[4,512,256]{2,1,0:T(8,128)S(1)}, u32[]{:S(2)}, u32[]{:S(2)}) async-start(f32[4,512,256]{2,1,0:T(8,128)} %all-reduce.5.cloned.1.call-done), calls=%async_computation.1 | async-start | bytes 4194304 | tf_op jit(solution)/shard_map/all_to_all | solution.py:49
  196.4 47.1 %all-to-all-done.1 = f32[4,512,256]{2,1,0:T(8,128)S(1)} async-done(((f32[4,512,256]{2,1,0:T(8,128)}), f32[4,512,256]{2,1,0:T(8,128)S(1)}, u32[]{:S(2)}, u32[]{:S(2)}) %all-to-all-start.1) | async-done | bytes 2097184 | tf_op jit(solution)/shard_map/all_to_all | solution.py:49
  243.5 1.5 multiply_bitcast_fusion
  245.1 1.9 copy.26
  247.0 141.5 %while.14 = (s32[]{:T(128)}, f32[512,1024]{0,1:T(8,128)S(1)}, s32[]{:T(128)}, s32[]{:T(128)}, f32[]{:T(128)}, /*index=5*/f32[]{:T(128)}, f32[]{:T(128)}, f32[]{:T(128)}, f32[]{:T(128)}) while((s32[]{:T(128)}, f32[512,1024]{0,1:T(8,128)S(1)}, s32[]{:T(128)}, s32[]{:T(128)}, f32[]{:T(128)}, /*index=5*/f32[]{:T(128)}, f32[]{:T(128)}, ...), condition=%wide.region_6.7_spmd.clone, body=%wide.region_1.6_spmd.clone.sunk | while | flops 13643786 | bytes 8453379 | solution.py:72
  247.0 0.6 multiply_reduce_fusion.2
  247.6 1.8 fusion.55
  249.5 1.0 fusion.57
  250.5 10.8 %all-reduce.2 = (f32[1024]{0:T(1024)S(1)}, f32[1024]{0:T(1024)S(1)}, f32[]{:T(128)}) all-reduce(f32[1024]{0:T(1024)S(1)} %bitcast.83, f32[1024]{0:T(1024)S(1)} %bitcast.84, f32[]{:T(128)} %get-tuple-element.117), channel_id=1, replica_groups=mesh['grp'=4,'inner'=8] {'grp'}, use_global_device_ids=true, to_apply=%region_5.5 | all-reduce | flops 2049 | bytes 16392 | tf_op jit(solution)/shard_map/while/body/eval_jaxpr/psum | solution.py:57
  261.3 0.7 dynamic_slice.24
  265.2 0.6 multiply_reduce_fusion.2
  265.8 1.8 fusion.55
  267.6 1.0 fusion.57
  268.7 9.9 %all-reduce.2 = (f32[1024]{0:T(1024)S(1)}, f32[1024]{0:T(1024)S(1)}, f32[]{:T(128)}) all-reduce(f32[1024]{0:T(1024)S(1)} %bitcast.83, f32[1024]{0:T(1024)S(1)} %bitcast.84, f32[]{:T(128)} %get-tuple-element.117), channel_id=1, replica_groups=mesh['grp'=4,'inner'=8] {'grp'}, use_global_device_ids=true, to_apply=%region_5.5 | all-reduce | flops 2049 | bytes 16392 | tf_op jit(solution)/shard_map/while/body/eval_jaxpr/psum | solution.py:57
  278.5 0.7 dynamic_slice.24
  282.4 0.6 multiply_reduce_fusion.2
  283.0 1.8 fusion.55
  284.9 1.0 fusion.57
  285.9 10.8 %all-reduce.2 = (f32[1024]{0:T(1024)S(1)}, f32[1024]{0:T(1024)S(1)}, f32[]{:T(128)}) all-reduce(f32[1024]{0:T(1024)S(1)} %bitcast.83, f32[1024]{0:T(1024)S(1)} %bitcast.84, f32[]{:T(128)} %get-tuple-element.117), channel_id=1, replica_groups=mesh['grp'=4,'inner'=8] {'grp'}, use_global_device_ids=true, to_apply=%region_5.5 | all-reduce | flops 2049 | bytes 16392 | tf_op jit(solution)/shard_map/while/body/eval_jaxpr/psum | solution.py:57
  296.7 0.7 dynamic_slice.24
  300.5 0.6 multiply_reduce_fusion.2
  301.1 1.8 fusion.55
  303.0 1.0 fusion.57
  304.0 9.9 %all-reduce.2 = (f32[1024]{0:T(1024)S(1)}, f32[1024]{0:T(1024)S(1)}, f32[]{:T(128)}) all-reduce(f32[1024]{0:T(1024)S(1)} %bitcast.83, f32[1024]{0:T(1024)S(1)} %bitcast.84, f32[]{:T(128)} %get-tuple-element.117), channel_id=1, replica_groups=mesh['grp'=4,'inner'=8] {'grp'}, use_global_device_ids=true, to_apply=%region_5.5 | all-reduce | flops 2049 | bytes 16392 | tf_op jit(solution)/shard_map/while/body/eval_jaxpr/psum | solution.py:57
  313.9 0.7 dynamic_slice.24
  317.8 0.6 multiply_reduce_fusion.2
  318.4 1.8 fusion.55
  320.2 1.0 fusion.57
  321.3 10.8 %all-reduce.2 = (f32[1024]{0:T(1024)S(1)}, f32[1024]{0:T(1024)S(1)}, f32[]{:T(128)}) all-reduce(f32[1024]{0:T(1024)S(1)} %bitcast.83, f32[1024]{0:T(1024)S(1)} %bitcast.84, f32[]{:T(128)} %get-tuple-element.117), channel_id=1, replica_groups=mesh['grp'=4,'inner'=8] {'grp'}, use_global_device_ids=true, to_apply=%region_5.5 | all-reduce | flops 2049 | bytes 16392 | tf_op jit(solution)/shard_map/while/body/eval_jaxpr/psum | solution.py:57
  332.1 0.7 dynamic_slice.24
  335.9 0.6 multiply_reduce_fusion.2
  336.5 1.8 fusion.55
  338.4 1.0 fusion.57
  339.4 9.9 %all-reduce.2 = (f32[1024]{0:T(1024)S(1)}, f32[1024]{0:T(1024)S(1)}, f32[]{:T(128)}) all-reduce(f32[1024]{0:T(1024)S(1)} %bitcast.83, f32[1024]{0:T(1024)S(1)} %bitcast.84, f32[]{:T(128)} %get-tuple-element.117), channel_id=1, replica_groups=mesh['grp'=4,'inner'=8] {'grp'}, use_global_device_ids=true, to_apply=%region_5.5 | all-reduce | flops 2049 | bytes 16392 | tf_op jit(solution)/shard_map/while/body/eval_jaxpr/psum | solution.py:57
  349.3 0.7 dynamic_slice.24
  353.2 0.6 multiply_reduce_fusion.2
  353.8 1.8 fusion.55
  355.6 1.0 fusion.57
  356.7 10.8 %all-reduce.2 = (f32[1024]{0:T(1024)S(1)}, f32[1024]{0:T(1024)S(1)}, f32[]{:T(128)}) all-reduce(f32[1024]{0:T(1024)S(1)} %bitcast.83, f32[1024]{0:T(1024)S(1)} %bitcast.84, f32[]{:T(128)} %get-tuple-element.117), channel_id=1, replica_groups=mesh['grp'=4,'inner'=8] {'grp'}, use_global_device_ids=true, to_apply=%region_5.5 | all-reduce | flops 2049 | bytes 16392 | tf_op jit(solution)/shard_map/while/body/eval_jaxpr/psum | solution.py:57
  367.4 0.7 dynamic_slice.24
  371.3 0.6 multiply_reduce_fusion.2
  371.9 1.8 fusion.55
  373.8 1.0 fusion.57
  374.8 9.9 %all-reduce.2 = (f32[1024]{0:T(1024)S(1)}, f32[1024]{0:T(1024)S(1)}, f32[]{:T(128)}) all-reduce(f32[1024]{0:T(1024)S(1)} %bitcast.83, f32[1024]{0:T(1024)S(1)} %bitcast.84, f32[]{:T(128)} %get-tuple-element.117), channel_id=1, replica_groups=mesh['grp'=4,'inner'=8] {'grp'}, use_global_device_ids=true, to_apply=%region_5.5 | all-reduce | flops 2049 | bytes 16392 | tf_op jit(solution)/shard_map/while/body/eval_jaxpr/psum | solution.py:57
  384.7 0.7 dynamic_slice.24
  388.5 1.8 copy.27
  (65 shorter events, 4.2 us)
Async XLA Ops:
  36.9 6.5 %copy-start = (s32[1,2048]{1,0:T(1,128)S(1)}, s32[1,2048]{1,0:T(1,128)}, u32[]{:S(2)}) copy-start(s32[1,2048]{1,0:T(1,128)} %param.7) | copy-start | bytes 24580
  36.9 54.7 %all-to-all-start = ((bf16[4,2,131072]{2,1,0:T(2,128)(2,1)}), bf16[4,2,131072]{2,1,0:T(2,128)(2,1)S(1)}, u32[]{:S(2)}, u32[]{:S(2)}) async-start(bf16[4,2,131072]{2,1,0:T(2,128)(2,1)} %reshape.93), calls=%async_computation | async-start | bytes 4194304 | tf_op jit(solution)/shard_map/all_to_all | solution.py:41
  43.4 148.5 %all-reduce.5.cloned.1.call-start = ((), (), s32[]{:S(2)}) async-start(), calls=%async_computation.2 | async-start | bytes 4194304 | tf_op jit(solution)/shard_map/psum | solution.py:48
  191.9 51.6 %all-to-all-start.1 = ((f32[4,512,256]{2,1,0:T(8,128)}), f32[4,512,256]{2,1,0:T(8,128)S(1)}, u32[]{:S(2)}, u32[]{:S(2)}) async-start(f32[4,512,256]{2,1,0:T(8,128)} %all-reduce.5.cloned.1.call-done), calls=%async_computation.1 | async-start | bytes 4194304 | tf_op jit(solution)/shard_map/all_to_all | solution.py:49
Sparse Core Ops, SparseCore 0:
  131.0 60.9 all-reduce.4
where the time goes:
time: 398 us; the launch traced here: 397 us
  waiting for transfers between devices  156 us (39%)
  blocking collectives  82.7 us (21%)
  local copies, waits for them, and re-layouts  56 us (14%)
  matrix products  28 us (7%)
  other arithmetic  27.4 us (7%)
  loops' own time  22.4 us (6%)
  between operations  13.5 us (3%)
  starting transfers between devices  11 us (3%)
    psum x8, blocking collectives, reflect(): lax.psum((jnp.sum(column * column), jnp.dot(column, current, precision=hi...  82.7 us
    psum x1, waiting for transfers between devices, on_device(): summed = lax.psum(partial_value, 'inner')  61.1 us
    all_to_all x1, waiting for transfers between devices, on_device(): lax.all_to_all(second_pass, 'grp', split_axis=2, concat_axis=1, tiled=True)  48.1 us
    all_to_all x1, waiting for transfers between devices, on_device(): lax.all_to_all(summed, 'grp', split_axis=0, concat_axis=1, tiled=True)  47.1 us
    another operation x1, loops' own time, on_device(): result = lax.fori_loop(0, COLS_DONE, reflect, sketch)  22.4 us
    gather x2, local copies, waits for them, and re-layouts, pick_rows(): return jnp.take(table_rows, chosen_rows, axis=0)  21.4 us
    dot_general x8, matrix products, reflect(): jnp.dot(column, current, precision=highest)  14.5 us
    unnamed x1, other arithmetic  12.8 us
  transfers between devices with their start and end apart: 3, of which 3 were waited for; matrix products, arithmetic and copies ran while one was open for 0% of the time, Pallas kernels for 0%

commit v1 on v0

--- a/solution.py
+++ b/solution.py
@@ -1,3 +1,4 @@
+import functools
 import math
 import jax
 import jax.numpy as jnp
@@ -6,6 +7,22 @@
 
 COLS_DONE = 8
 epsilon = 1e-06
+
+
+def process_slices(local_values, mesh_name):
+    many = lax.axis_size(mesh_name)
+
+    def cut_screen(mixed_arr, w1):
+        if w1 >= many:
+            return mixed_arr
+        built = tuple(((to_i, to_i ^ w1) for to_i in range(many)))
+        opened = lax.ppermute(mixed_arr, axis_name=mesh_name, perm=built)
+        return cut_screen(mixed_arr + opened, 2 * w1)
+
+    return cut_screen(local_values, 1)
+
+
+_create_task = functools.partial(process_slices, mesh_name="inner")
 
 
 def sign_table(row_ids, col_ids):
@@ -45,7 +62,7 @@
     mixed_rows = mixed_rows.reshape(block_count, 16 * 256, col_count)
     picked = jax.vmap(pick_rows)(mixed_rows, kept_rows)
     partial_value = jnp.sum(picked, axis=0)
-    summed = lax.psum(partial_value, "inner")
+    summed = _create_task(partial_value)
     sketch = lax.all_to_all(summed, "grp", split_axis=0, concat_axis=1, tiled=True)
     sketch = sketch * (1.0 / (64.0 * math.sqrt(keep_count)))
     row_base = lax.axis_index("grp") * owned_rows

time: 398 us -> 422 us (1.060)
  waiting for transfers between devices: 156 us -> 191 us
  between operations: 13.5 us -> 0.13 us
    ppermute x0 -> x3, waiting for transfers between devices: none -> 95.5 us  [cut_screen(): opened = lax.ppermute(mixed_arr, axis_name=mesh_name, perm=built)]
    psum x1 -> x0, waiting for transfers between devices: 61.1 us -> none  [on_device(): summed = lax.psum(partial_value, 'inner')]
  transfers between devices with their start and end apart: 3 -> 5, of which waited for: 3 -> 5; matrix products, arithmetic and copies ran while one was open for 0% -> 0% of each run, Pallas kernels for 0% -> 0%
where the time goes in v1:
time: 422 us; the launch traced here: 420 us
  waiting for transfers between devices  191 us (45%)
  blocking collectives  82.7 us (20%)
  local copies, waits for them, and re-layouts  55.6 us (13%)
  other arithmetic  28.4 us (7%)
  matrix products  28 us (7%)
  loops' own time  21.5 us (5%)
  starting transfers between devices  13.5 us (3%)
    ppermute x3, waiting for transfers between devices, cut_screen(): opened = lax.ppermute(mixed_arr, axis_name=mesh_name, perm=built)  95.5 us
    psum x8, blocking collectives, reflect(): lax.psum((jnp.sum(column * column), jnp.dot(column, current, precision=hi...  82.7 us
    all_to_all x1, waiting for transfers between devices, on_device(): lax.all_to_all(second_pass, 'grp', split_axis=2, concat_axis=1, tiled=True)  48.1 us
    all_to_all x1, waiting for transfers between devices, on_device(): lax.all_to_all(summed, 'grp', split_axis=0, concat_axis=1, tiled=True)  47 us
    another operation x1, loops' own time, on_device(): result = lax.fori_loop(0, COLS_DONE, reflect, sketch)  21.5 us
    gather x2, local copies, waits for them, and re-layouts, pick_rows(): return jnp.take(table_rows, chosen_rows, axis=0)  21.4 us
    dot_general x8, matrix products, reflect(): jnp.dot(column, current, precision=highest)  14.5 us
    unnamed x1, other arithmetic  12.8 us
  transfers between devices with their start and end apart: 5, of which 5 were waited for; matrix products, arithmetic and copies ran while one was open for 0% of the time, Pallas kernels for 0%

profile of v1, /device:TPU:0, one launch (start us, length us, event | category | flops | bytes accessed | tf_op | source)
XLA Modules:
  0.0 420.3 jit_solution(4067087129136731576)
XLA Ops:
  0.0 0.7 subtract_convert_fusion.4
  0.7 2.5 multiply_convert_fusion
  3.2 0.7 convolution_convert_fusion
  3.9 1.5 convert_bitcast_fusion
  5.4 1.2 copy.21
  6.6 7.7 %copy.22 = bf16[1,1024,1024]{1,0,2:T(2,128)(2,1)} copy(bf16[1,1024,1024]{2,1,0:T(8,128)(2,1)S(1)} %bitcast.77) | data formatting | bytes 4194304 | tf_op jit(solution)/shard_map/reshape | solution.py:57
  14.8 12.8 %reduce.2 = bf16[1024,1024]{1,0:T(8,128)(2,1)S(1)} reduce(bf16[1024,1,1024]{2,1,0:T(2,128)(2,1)} %bitcast.75, bf16[]{:T(256)} %broadcast.106), dimensions={1}, to_apply=%bitcast.43.reduce_sub_computation | reduce | bytes 4194306
  27.6 2.8 reshape.93
  30.4 6.5 %all-to-all-start = ((bf16[4,2,131072]{2,1,0:T(2,128)(2,1)}), bf16[4,2,131072]{2,1,0:T(2,128)(2,1)S(1)}, u32[]{:S(2)}, u32[]{:S(2)}) async-start(bf16[4,2,131072]{2,1,0:T(2,128)(2,1)} %reshape.93), calls=%async_computation | async-start | bytes 4194304 | tf_op jit(solution)/shard_map/all_to_all | solution.py:58
  37.0 48.1 %all-to-all-done = bf16[4,2,131072]{2,1,0:T(2,128)(2,1)S(1)} async-done(((bf16[4,2,131072]{2,1,0:T(2,128)(2,1)}), bf16[4,2,131072]{2,1,0:T(2,128)(2,1)S(1)}, u32[]{:S(2)}, u32[]{:S(2)}) %all-to-all-start) | async-done | bytes 2097184 | tf_op jit(solution)/shard_map/all_to_all | solution.py:58
  85.1 3.4 reshape.94
  88.4 3.0 copy.29
  91.4 2.6 copy.23
  94.0 2.9 convolution_bitcast_fusion
  96.9 4.4 %copy.25 = f32[1,16,256,256]{3,2,1,0:T(8,128)} copy(f32[1,16,256,256]{3,1,2,0:T(8,128)S(1)} %convolution_bitcast_fusion) | data formatting | bytes 8388608 | tf_op jit(solution)/shard_map/ha,nakd->nhkd/transpose | solution.py:61
  101.3 21.4 %gather_fusion = f32[2048,256]{1,0:T(8,128)S(1)} fusion(f32[1,4096,256]{2,1,0:T(8,128)} %bitcast.74, s32[2048]{0:T(1024)S(1)} %bitcast.73), kind=kCustom, calls=%fused_computation | custom fusion | bytes 4210688 | tf_op jit(solution)/shard_map/vmap(jit(_take))/gather | solution.py:37
  123.1 4.1 collective-permute-done
  127.7 1.6 collective-permute-start.1
  129.3 46.1 %collective-permute-done.1 = f32[2048,256]{1,0:T(8,128)S(1)} collective-permute-done((f32[2048,256]{1,0:T(8,128)S(1)}, f32[2048,256]{1,0:T(8,128)S(1)}, u32[]{:S(2)}, u32[]{:S(2)}) %collective-permute-start.1) | collective-permute-done | bytes 2097184 | tf_op jit(solution)/shard_map/ppermute | solution.py:19
  175.7 1.6 collective-permute-start.2
  177.3 45.2 %collective-permute-done.2 = f32[2048,256]{1,0:T(8,128)S(1)} collective-permute-done((f32[2048,256]{1,0:T(8,128)S(1)}, f32[2048,256]{1,0:T(8,128)S(1)}, u32[]{:S(2)}, u32[]{:S(2)}) %collective-permute-start.2) | collective-permute-done | bytes 2097184 | tf_op jit(solution)/shard_map/ppermute | solution.py:19
  222.5 1.6 add.86
  224.1 3.6 all-to-all-start.1
  227.8 47.0 %all-to-all-done.1 = f32[4,512,256]{2,1,0:T(8,128)S(1)} async-done(((f32[4,512,256]{2,1,0:T(8,128)}), f32[4,512,256]{2,1,0:T(8,128)S(1)}, u32[]{:S(2)}, u32[]{:S(2)}) %all-to-all-start.1) | async-done | bytes 2097184 | tf_op jit(solution)/shard_map/all_to_all | solution.py:66
  274.8 1.5 multiply_bitcast_fusion
  276.3 1.9 copy.26
  278.2 140.2 %while.14 = (s32[]{:T(128)}, f32[512,1024]{0,1:T(8,128)S(1)}, s32[]{:T(128)}, s32[]{:T(128)}, f32[]{:T(128)}, /*index=5*/f32[]{:T(128)}, f32[]{:T(128)}, f32[]{:T(128)}, f32[]{:T(128)}) while((s32[]{:T(128)}, f32[512,1024]{0,1:T(8,128)S(1)}, s32[]{:T(128)}, s32[]{:T(128)}, f32[]{:T(128)}, /*index=5*/f32[]{:T(128)}, f32[]{:T(128)}, ...), condition=%wide.region_5.6_spmd.clone, body=%wide.region_0.5_spmd.clone.sunk | while | flops 13643786 | bytes 8453379 | solution.py:89
  278.3 0.6 multiply_reduce_fusion.2
  278.9 1.8 fusion.56
  280.7 1.0 fusion.58
  281.8 10.8 %all-reduce.2 = (f32[1024]{0:T(1024)S(1)}, f32[1024]{0:T(1024)S(1)}, f32[]{:T(128)}) all-reduce(f32[1024]{0:T(1024)S(1)} %bitcast.82, f32[1024]{0:T(1024)S(1)} %bitcast.83, f32[]{:T(128)} %get-tuple-element.117), channel_id=1, replica_groups=mesh['grp'=4,'inner'=8] {'grp'}, use_global_device_ids=true, to_apply=%region_4.4 | all-reduce | flops 2049 | bytes 16392 | tf_op jit(solution)/shard_map/while/body/eval_jaxpr/psum | solution.py:74
  292.6 0.6 dynamic_slice.24
  296.2 0.6 multiply_reduce_fusion.2
  296.9 1.8 fusion.56
  298.7 1.0 fusion.58
  299.7 9.9 %all-reduce.2 = (f32[1024]{0:T(1024)S(1)}, f32[1024]{0:T(1024)S(1)}, f32[]{:T(128)}) all-reduce(f32[1024]{0:T(1024)S(1)} %bitcast.82, f32[1024]{0:T(1024)S(1)} %bitcast.83, f32[]{:T(128)} %get-tuple-element.117), channel_id=1, replica_groups=mesh['grp'=4,'inner'=8] {'grp'}, use_global_device_ids=true, to_apply=%region_4.4 | all-reduce | flops 2049 | bytes 16392 | tf_op jit(solution)/shard_map/while/body/eval_jaxpr/psum | solution.py:74
  309.6 0.6 dynamic_slice.24
  313.3 0.6 multiply_reduce_fusion.2
  313.9 1.8 fusion.56
  315.8 1.0 fusion.58
  316.8 10.8 %all-reduce.2 = (f32[1024]{0:T(1024)S(1)}, f32[1024]{0:T(1024)S(1)}, f32[]{:T(128)}) all-reduce(f32[1024]{0:T(1024)S(1)} %bitcast.82, f32[1024]{0:T(1024)S(1)} %bitcast.83, f32[]{:T(128)} %get-tuple-element.117), channel_id=1, replica_groups=mesh['grp'=4,'inner'=8] {'grp'}, use_global_device_ids=true, to_apply=%region_4.4 | all-reduce | flops 2049 | bytes 16392 | tf_op jit(solution)/shard_map/while/body/eval_jaxpr/psum | solution.py:74
  327.6 0.6 dynamic_slice.24
  331.3 0.6 multiply_reduce_fusion.2
  331.9 1.8 fusion.56
  333.8 1.0 fusion.58
  334.8 9.9 %all-reduce.2 = (f32[1024]{0:T(1024)S(1)}, f32[1024]{0:T(1024)S(1)}, f32[]{:T(128)}) all-reduce(f32[1024]{0:T(1024)S(1)} %bitcast.82, f32[1024]{0:T(1024)S(1)} %bitcast.83, f32[]{:T(128)} %get-tuple-element.117), channel_id=1, replica_groups=mesh['grp'=4,'inner'=8] {'grp'}, use_global_device_ids=true, to_apply=%region_4.4 | all-reduce | flops 2049 | bytes 16392 | tf_op jit(solution)/shard_map/while/body/eval_jaxpr/psum | solution.py:74
  344.7 0.6 dynamic_slice.24
  349.0 1.8 fusion.56
  350.8 1.0 fusion.58
  351.9 10.8 %all-reduce.2 = (f32[1024]{0:T(1024)S(1)}, f32[1024]{0:T(1024)S(1)}, f32[]{:T(128)}) all-reduce(f32[1024]{0:T(1024)S(1)} %bitcast.82, f32[1024]{0:T(1024)S(1)} %bitcast.83, f32[]{:T(128)} %get-tuple-element.117), channel_id=1, replica_groups=mesh['grp'=4,'inner'=8] {'grp'}, use_global_device_ids=true, to_apply=%region_4.4 | all-reduce | flops 2049 | bytes 16392 | tf_op jit(solution)/shard_map/while/body/eval_jaxpr/psum | solution.py:74
  362.7 0.6 dynamic_slice.24
  367.0 1.8 fusion.56
  368.8 1.0 fusion.58
  369.9 9.9 %all-reduce.2 = (f32[1024]{0:T(1024)S(1)}, f32[1024]{0:T(1024)S(1)}, f32[]{:T(128)}) all-reduce(f32[1024]{0:T(1024)S(1)} %bitcast.82, f32[1024]{0:T(1024)S(1)} %bitcast.83, f32[]{:T(128)} %get-tuple-element.117), channel_id=1, replica_groups=mesh['grp'=4,'inner'=8] {'grp'}, use_global_device_ids=true, to_apply=%region_4.4 | all-reduce | flops 2049 | bytes 16392 | tf_op jit(solution)/shard_map/while/body/eval_jaxpr/psum | solution.py:74
  379.7 0.6 dynamic_slice.24
  384.0 1.8 fusion.56
  385.9 1.0 fusion.58
  386.9 11.0 %all-reduce.2 = (f32[1024]{0:T(1024)S(1)}, f32[1024]{0:T(1024)S(1)}, f32[]{:T(128)}) all-reduce(f32[1024]{0:T(1024)S(1)} %bitcast.82, f32[1024]{0:T(1024)S(1)} %bitcast.83, f32[]{:T(128)} %get-tuple-element.117), channel_id=1, replica_groups=mesh['grp'=4,'inner'=8] {'grp'}, use_global_device_ids=true, to_apply=%region_4.4 | all-reduce | flops 2049 | bytes 16392 | tf_op jit(solution)/shard_map/while/body/eval_jaxpr/psum | solution.py:74
  397.9 0.6 dynamic_slice.24
  402.2 1.8 fusion.56
  404.1 1.0 fusion.58
  405.1 9.7 %all-reduce.2 = (f32[1024]{0:T(1024)S(1)}, f32[1024]{0:T(1024)S(1)}, f32[]{:T(128)}) all-reduce(f32[1024]{0:T(1024)S(1)} %bitcast.82, f32[1024]{0:T(1024)S(1)} %bitcast.83, f32[]{:T(128)} %get-tuple-element.117), channel_id=1, replica_groups=mesh['grp'=4,'inner'=8] {'grp'}, use_global_device_ids=true, to_apply=%region_4.4 | all-reduce | flops 2049 | bytes 16392 | tf_op jit(solution)/shard_map/while/body/eval_jaxpr/psum | solution.py:74
  414.8 0.6 dynamic_slice.24
  418.5 1.8 copy.27
  (71 shorter events, 7.7 us)
Async XLA Ops:
  30.4 6.5 %copy-start = (s32[1,2048]{1,0:T(1,128)S(1)}, s32[1,2048]{1,0:T(1,128)}, u32[]{:S(2)}) copy-start(s32[1,2048]{1,0:T(1,128)} %param.7) | copy-start | bytes 24580
  30.4 54.7 %all-to-all-start = ((bf16[4,2,131072]{2,1,0:T(2,128)(2,1)}), bf16[4,2,131072]{2,1,0:T(2,128)(2,1)S(1)}, u32[]{:S(2)}, u32[]{:S(2)}) async-start(bf16[4,2,131072]{2,1,0:T(2,128)(2,1)} %reshape.93), calls=%async_computation | async-start | bytes 4194304 | tf_op jit(solution)/shard_map/all_to_all | solution.py:58
  123.0 4.2 %collective-permute-start = (f32[2048,256]{1,0:T(8,128)S(1)}, f32[2048,256]{1,0:T(8,128)S(1)}, u32[]{:S(2)}, u32[]{:S(2)}) collective-permute-start(f32[2048,256]{1,0:T(8,128)S(1)} %broadcast_select_fusion.2), channel_id=1, source_target_pairs={{0,1},{1,0},{2,3},{3,2},{4,5},{5,4},{6,7},{7,6},{8,9},{9,8},{10,11... | collective-permute-start | bytes 6291464 | tf_op jit(solution)/shard_map/ppermute | solution.py:19
  127.7 47.7 %collective-permute-start.1 = (f32[2048,256]{1,0:T(8,128)S(1)}, f32[2048,256]{1,0:T(8,128)S(1)}, u32[]{:S(2)}, u32[]{:S(2)}) collective-permute-start(f32[2048,256]{1,0:T(8,128)S(1)} %fusion.43), channel_id=1, source_target_pairs={{0,2},{1,3},{2,0},{3,1},{4,6},{5,7},{6,4},{7,5},{8,10},{9,11},{10,... | collective-permute-start | bytes 6291464 | tf_op jit(solution)/shard_map/ppermute | solution.py:19
  175.7 46.9 %collective-permute-start.2 = (f32[2048,256]{1,0:T(8,128)S(1)}, f32[2048,256]{1,0:T(8,128)S(1)}, u32[]{:S(2)}, u32[]{:S(2)}) collective-permute-start(f32[2048,256]{1,0:T(8,128)S(1)} %add.85), channel_id=1, source_target_pairs={{0,4},{1,5},{2,6},{3,7},{4,0},{5,1},{6,2},{7,3},{8,12},{9,13},{10,... | collective-permute-start | bytes 6291464 | tf_op jit(solution)/shard_map/ppermute | solution.py:19
  224.1 50.6 %all-to-all-start.1 = ((f32[4,512,256]{2,1,0:T(8,128)}), f32[4,512,256]{2,1,0:T(8,128)S(1)}, u32[]{:S(2)}, u32[]{:S(2)}) async-start(f32[4,512,256]{2,1,0:T(8,128)} %bitcast.17), calls=%async_computation.1 | async-start | bytes 4194304 | tf_op jit(solution)/shard_map/all_to_all | solution.py:66
